TPU v7x, 256 devices: a whole 4x4x8 slice. The times are simulated.
256 devices in a mesh: section: 8 (over z_lo, core), vocab: 32 (over y, z_hi, x).
Axes of the slice: x: 4, y: 4, z: 8 (z_hi: 2, z_lo: 4; z = z_hi * 4 + z_lo), core: 2. Of those that a mesh axis runs over, the one named last changes fastest.
Arguments:
- hidden: bfloat16 [8, 512, 8192], P('section', None, 'vocab'), may hold values from -160 to 160
- final_hidden: bfloat16 [512, 8192], P('section', 'vocab'), may hold values from -160 to 160
- row_pick: int32 [8, 128], P('section'), may hold values from 0 to 511
- trans_weight: bfloat16 [8, 8192, 8192], P('section', None, 'vocab'), may hold values from -0.0625 to 0.0625
- trans_bias: bfloat16 [8, 8192], P('section', 'vocab'), may hold values from -6 to 6
- norm_gain: bfloat16 [8192], P('vocab'), may hold values from 0.5 to 1.5
- unembed: bfloat16 [8192, 16384], P('section', 'vocab'), may hold values from -100 to 100
Outputs:
- grad_weight: bfloat16 [8, 8192, 8192], P('section', None, 'vocab')
- grad_bias: float32 [8, 8192], P('section', 'vocab')
- kl_mean: float32 [8], P('section')
All inputs are finite; a program needn't handle non-finite values.
Results may differ from a plain program's by a relative error of at most 0.024.
Values may be sent and summed in bfloat16 or wider, within the bound.
A program may use at most 64 MiB of HBM per device.

v0:
```python
import jax
import jax.numpy as jnp
from jax import lax
from jax.sharding import PartitionSpec as P

epsilon = 1e-05


def combined_all(value, axis, join):
    pieces = jax.tree.map(lambda part: lax.all_gather(part, axis), value)
    head = jax.tree.map(lambda part: part[0], pieces)
    tail = jax.tree.map(lambda part: part[1:], pieces)
    so_far, _ = lax.scan(lambda so_far, section: (join(so_far, section), None), head, tail)
    return so_far


def combine_totals(first, second):
    trans_max = jnp.maximum(first[0], second[0])
    trans_sum = first[1] * jnp.exp(first[0] - trans_max) + second[1] * jnp.exp(
        second[0] - trans_max
    )
    target_max = jnp.maximum(first[2], second[2])
    target_sum = first[3] * jnp.exp(first[2] - target_max) + second[3] * jnp.exp(
        second[2] - target_max
    )
    return (trans_max, trans_sum, target_max, target_sum)


def local_totals(logits):
    highest = jnp.max(logits, axis=-1)
    return (highest, jnp.sum(jnp.exp(logits - highest[:, None]), axis=-1))


def per_device(hidden, final_hidden, row_pick, trans_weight, trans_bias, norm_gain, unembed):
    gain_cols = norm_gain.astype(jnp.float32)
    width = trans_weight.shape[1]
    row_count = row_pick.shape[1]
    unembed_full = lax.all_gather(unembed, "section", axis=0, tiled=True)
    final_cols = lax.all_gather(final_hidden, "section", axis=0, tiled=True)
    picked = row_pick[0]
    input_cols = hidden[0][picked]
    inputs = lax.all_gather(input_cols, "vocab", axis=1, tiled=True)
    trans = (
        input_cols.astype(jnp.float32)
        + jnp.dot(inputs, trans_weight[0], preferred_element_type=jnp.float32)
        + trans_bias[0].astype(jnp.float32)
    )
    finals = final_cols[picked].astype(jnp.float32)
    trans_total, final_total = lax.psum(
        (jnp.sum(trans * trans, axis=-1), jnp.sum(finals * finals, axis=-1)), "vocab"
    )
    trans_scale = lax.rsqrt(trans_total / width + epsilon)
    final_scale = lax.rsqrt(final_total / width + epsilon)
    normed = (trans * trans_scale[:, None] * gain_cols).astype(jnp.bfloat16)
    target = (finals * final_scale[:, None] * gain_cols).astype(jnp.bfloat16)
    slab_rows = unembed_full
    logits = jnp.dot(
        lax.all_gather(normed, "vocab", axis=1, tiled=True),
        slab_rows,
        preferred_element_type=jnp.float32,
    )
    target_logits = jnp.dot(
        lax.all_gather(target, "vocab", axis=1, tiled=True),
        slab_rows,
        preferred_element_type=jnp.float32,
    )
    trans_max, trans_sum = local_totals(logits)
    target_max, target_sum = local_totals(target_logits)
    totals = combined_all((trans_max, trans_sum, target_max, target_sum), "vocab", combine_totals)
    log_trans = logits - (totals[0] + jnp.log(totals[1]))[:, None]
    log_target = target_logits - (totals[2] + jnp.log(totals[3]))[:, None]
    probs = jnp.exp(log_target)
    kl_part = jnp.sum(probs * (log_target - log_trans), axis=-1)
    dlogits = (jnp.exp(log_trans) - probs).astype(jnp.bfloat16)
    kl_rows = lax.psum(kl_part, "vocab")
    slab_rows = unembed_full
    dnormed_cols = lax.psum_scatter(
        lax.dot_general(
            slab_rows, dlogits, (((1,), (1,)), ((), ())), preferred_element_type=jnp.float32
        ).astype(jnp.bfloat16),
        "vocab",
        scatter_dimension=0,
        tiled=True,
    ).astype(jnp.float32)
    trans_cols = trans.T
    scaled_cols = dnormed_cols * gain_cols[:, None]
    product = lax.psum(jnp.sum(scaled_cols * trans_cols, axis=0), "vocab") / width
    dtrans_cols = trans_scale[None, :] * (
        scaled_cols - trans_cols * (trans_scale * trans_scale * product)[None, :]
    )
    grad_weights = [
        lax.dot_general(
            inputs,
            dtrans_cols.astype(jnp.bfloat16),
            (((0,), (1,)), ((), ())),
            preferred_element_type=jnp.float32,
        ).astype(jnp.bfloat16)
    ]
    grad_biases = [jnp.sum(dtrans_cols, axis=1)]
    kl_values = [jnp.sum(kl_rows) / row_count]
    return (jnp.stack(grad_weights), jnp.stack(grad_biases), jnp.stack(kl_values))


def solution(mesh):
    placed = (
        P("section", None, "vocab"),
        P("section", "vocab"),
        P("section", None),
        P("section", None, "vocab"),
        P("section", "vocab"),
        P("vocab"),
        P("section", "vocab"),
    )
    return jax.shard_map(
        per_device,
        mesh=mesh,
        in_specs=placed,
        out_specs=(P("section", None, "vocab"), P("section", "vocab"), P("section")),
        check_vma=False,
    )
```

profile of v0, /device:TPU:2, one launch (start us, length us, event | category | flops | bytes accessed | tf_op | source)
XLA Modules:
  0.0 1215.9 jit_solution(14653384392186049527)
XLA Ops:
  7.2 0.0 copy-start
  7.2 0.0 all-gather.20.cloned.1.call-start
  7.2 0.7 fusion.34
  7.9 0.2 copy-done
  8.1 1.5 gather_fusion
  9.6 0.0 all-gather.20.cloned.1.call-update
  9.6 0.0 all-gather.14.cloned.1.call-start
  9.7 0.7 add.75
  10.4 0.7 convert_element_type.38
  11.0 15.4 %all_gather.46 = bf16[512,256]{1,0:T(8,128)(2,1)S(1)} all-gather(bf16[64,256]{1,0:T(8,128)(2,1)} %param.10), channel_id=1, replica_groups=mesh['section'=8,'vocab'=32] {'section'}, dimensions={0}, use_global_device_ids=true | all-gather | bytes 294912 | tf_op jit(solution)/shard_map/all_gather | solution.py:39
  26.4 0.8 gather_fusion.1
  27.2 0.1 fusion.20
  27.3 84.5 %all-gather.20.cloned.1.call-done = bf16[128,8192]{1,0:T(8,128)(2,1)} async-done(((bf16[128,256]{1,0:T(8,128)(2,1)}), bf16[128,8192]{1,0:T(8,128)(2,1)}) %all-gather.20.cloned.1.call-update) | async-done | bytes 2097168 | tf_op jit(solution)/shard_map/all_gather | solution.py:42
  111.8 3.7 multiply_reduce_fusion.1
  115.4 109.8 %all-reduce.1 = (f32[128]{0:T(128)S(1)}, f32[128]{0:T(128)S(1)}) all-reduce(f32[128]{0:T(128)S(1)} %fusion.20, f32[128]{0:T(128)S(1)} %get-tuple-element.87), channel_id=1, replica_groups=mesh['section'=8,'vocab'=32] {'vocab'}, use_global_device_ids=true, to_apply=%region_5.0 | all-reduce | flops 256 | bytes 2048 | tf_op jit(solution)/shard_map/psum | solution.py:49
  225.3 0.8 multiply_convert_fusion
  226.1 0.0 all-gather.14.cloned.1.call-update
  226.1 0.0 all-gather.16.cloned.1.call-start
  226.1 0.7 all-gather.16.cloned.1.call-update
  226.8 0.0 all-gather.18.cloned.1.call-start
  226.9 0.5 all-gather.18.cloned.1.call-update
  227.4 0.0 reduce-scatter.2.cloned.1.call-start
  227.4 90.7 %all-gather.14.cloned.1.call-done = bf16[128,8192]{1,0:T(8,128)(2,1)} async-done(((bf16[128,256]{1,0:T(8,128)(2,1)}), bf16[128,8192]{1,0:T(8,128)(2,1)}) %all-gather.14.cloned.1.call-update) | async-done | bytes 2097168 | tf_op jit(solution)/shard_map/all_gather | solution.py:58
  318.2 91.2 %all-gather.16.cloned.1.call-done = bf16[8192,512]{1,0:T(8,128)(2,1)} async-done(((bf16[1024,512]{1,0:T(8,128)(2,1)}), bf16[8192,512]{1,0:T(8,128)(2,1)}) %all-gather.16.cloned.1.call-update) | async-done | bytes 8388624 | tf_op jit(solution)/shard_map/all_gather | solution.py:38
  409.4 5.4 fusion.37
  414.8 107.7 %all-gather.5 = f32[32,1,128]{2,1,0:T(1,128)S(1)} all-gather(f32[1,1,128]{2,1,0:T(1,128)S(1)} %bitcast.100), channel_id=3, replica_groups=mesh['section'=8,'vocab'=32] {'vocab'}, dimensions={0}, use_global_device_ids=true | all-gather | bytes 16896 | tf_op jit(solution)/shard_map/all_gather | solution.py:10
  522.5 0.2 exponential_reduce_fusion.1
  522.6 115.5 %all-gather.6 = f32[32,1,128]{2,1,0:T(1,128)S(1)} all-gather(f32[1,1,128]{2,1,0:T(1,128)S(1)} %bitcast.102), channel_id=4, replica_groups=mesh['section'=8,'vocab'=32] {'vocab'}, dimensions={0}, use_global_device_ids=true | all-gather | bytes 16896 | tf_op jit(solution)/shard_map/all_gather | solution.py:10
  638.2 0.0 all-gather.18.cloned.1.call-done
  638.2 5.4 fusion.38
  643.6 106.6 %all-gather.7 = f32[32,1,128]{2,1,0:T(1,128)S(1)} all-gather(f32[1,1,128]{2,1,0:T(1,128)S(1)} %bitcast.99), channel_id=5, replica_groups=mesh['section'=8,'vocab'=32] {'vocab'}, dimensions={0}, use_global_device_ids=true | all-gather | bytes 16896 | tf_op jit(solution)/shard_map/all_gather | solution.py:10
  750.1 0.2 exponential_reduce_fusion
  750.3 108.6 %all-gather.8 = f32[32,1,128]{2,1,0:T(1,128)S(1)} all-gather(f32[1,1,128]{2,1,0:T(1,128)S(1)} %bitcast.103), channel_id=6, replica_groups=mesh['section'=8,'vocab'=32] {'vocab'}, dimensions={0}, use_global_device_ids=true | all-gather | bytes 16896 | tf_op jit(solution)/shard_map/all_gather | solution.py:10
  858.9 1.5 while.16
  860.5 7.5 fusion.11
  868.0 0.0 copy-start.1
  868.0 0.0 reduce-scatter.2.cloned.1.call-update
  868.0 0.2 multiply_reduce_fusion
  868.3 214.5 %reduce-scatter.2.cloned.1.call-done = bf16[256,128]{0,1:T(8,128)(2,1)} async-done(((bf16[8192,128]{0,1:T(8,128)(2,1)}), bf16[256,128]{0,1:T(8,128)(2,1)}) %reduce-scatter.2.cloned.1.call-update) | async-done | bytes 65552 | tf_op jit(solution)/shard_map/reduce_scatter | solution.py:77
  1082.8 0.0 copy-start.2
  1082.8 1.0 fusion.23
  1083.8 118.2 %all-reduce = (f32[128]{0:T(128)S(1)}, f32[128]{0:T(128)S(1)}) all-reduce(f32[128]{0:T(128)S(1)} %fusion.23, f32[128]{0:T(128)S(1)} %multiply_reduce_fusion), channel_id=1, replica_groups=mesh['section'=8,'vocab'=32] {'vocab'}, use_global_device_ids=true, to_apply=%region_12.13 | all-reduce | flops 256 | bytes 2048 | tf_op jit(solution)/shard_map/psum | solution.py:87
  1202.1 0.6 reduce_sum.79
  1203.3 0.0 copy-done.1
  1203.4 4.2 fusion.10
  1207.5 0.0 copy-done.2
  1207.5 0.7 fusion.28
  (48 shorter events, 1.1 us)
Async XLA Ops:
  7.2 1.0 copy-start
  7.2 104.6 %all-gather.20.cloned.1.call-start = ((), (), s32[]{:S(2)}) async-start(), calls=%async_computation.5 | async-start | bytes 2162688 | tf_op jit(solution)/shard_map/all_gather | solution.py:42
  9.6 308.6 %all-gather.14.cloned.1.call-start = ((), (), s32[]{:S(2)}) async-start(), calls=%async_computation.1 | async-start | bytes 2162688 | tf_op jit(solution)/shard_map/all_gather | solution.py:58
  226.1 183.3 %all-gather.16.cloned.1.call-start = ((), (), s32[]{:S(2)}) async-start(), calls=%async_computation.2 | async-start | bytes 9437184 | tf_op jit(solution)/shard_map/all_gather | solution.py:38
  226.8 411.4 %all-gather.18.cloned.1.call-start = ((), (), s32[]{:S(2)}) async-start(), calls=%async_computation.3 | async-start | bytes 2162688 | tf_op jit(solution)/shard_map/all_gather | solution.py:63
  227.4 855.4 %reduce-scatter.2.cloned.1.call-start = ((), (), s32[]{:S(2)}) async-start(), calls=%async_computation.4 | async-start | bytes 2162688 | tf_op jit(solution)/shard_map/reduce_scatter | solution.py:77
  868.0 335.3 %copy-start.1 = (bf16[128,8192]{1,0:T(8,128)(2,1)S(1)}, bf16[128,8192]{1,0:T(8,128)(2,1)}, u32[]{:S(2)}) copy-start(bf16[128,8192]{1,0:T(8,128)(2,1)} %all-gather.20.cloned.1.call-done) | copy-start | bytes 6291460
  1082.8 124.7 %copy-start.2 = (bf16[256,128]{0,1:T(8,128)(2,1)S(1)}, bf16[256,128]{0,1:T(8,128)(2,1)}, u32[]{:S(2)}) copy-start(bf16[256,128]{0,1:T(8,128)(2,1)} %reduce-scatter.2.cloned.1.call-done) | copy-start | bytes 196612
Sparse Core Ops, SparseCore 0:
  11.8 99.9 all-gather.19
  226.2 91.9 all-gather.13
  320.0 89.4 all-gather.15
  412.5 95.5 all-gather.17
  868.2 214.5 reduce-scatter.1
where the time goes:
time: 1220 us
  blocking collectives  682 us (56%)
  waiting for transfers between devices  482 us (40%)
  matrix products  26.1 us (2%)
  between operations  15.7 us (1%)
    all_gather x4, blocking collectives, combined_all(): pieces = jax.tree.map(lambda part: lax.all_gather(part, axis), value)  438 us
    reduce_scatter x1, waiting for transfers between devices, per_device(): lax.psum_scatter(lax.dot_general(slab_rows, dlogits, (((1,), (1,)), ((),...  215 us
    psum x1, blocking collectives, per_device(): lax.psum(jnp.sum(scaled_cols * trans_cols, axis=0), 'vocab') / width  118 us
    psum x1, blocking collectives, per_device(): lax.psum((jnp.sum(trans * trans, axis=-1), jnp.sum(finals * finals, axis=...  110 us
    all_gather x1, waiting for transfers between devices, per_device(): unembed_full = lax.all_gather(unembed, 'section', axis=0, tiled=True)  91.2 us
    all_gather x1, waiting for transfers between devices, per_device(): lax.all_gather(normed, 'vocab', axis=1, tiled=True)  90.7 us
    all_gather x1, waiting for transfers between devices, per_device(): inputs = lax.all_gather(input_cols, 'vocab', axis=1, tiled=True)  84.5 us
  transfers between devices with their start and end apart: 5, of which 4 were waited for; matrix products, arithmetic and copies ran while one was open for 1% of the time, Pallas kernels for 0%

commit v1 on v0

--- a/solution.py
+++ b/solution.py
@@ -32,6 +32,12 @@
 
 
 def per_device(hidden, final_hidden, row_pick, trans_weight, trans_bias, norm_gain, unembed):
+
+    def modes_switch(body):
+        return jnp.concatenate(
+            lax.all_to_all(jnp.stack(lax.axis_size("vocab") * [body], 0), "vocab", 0, 0), 1
+        )
+
     gain_cols = norm_gain.astype(jnp.float32)
     width = trans_weight.shape[1]
     row_count = row_pick.shape[1]
@@ -54,11 +60,7 @@
     normed = (trans * trans_scale[:, None] * gain_cols).astype(jnp.bfloat16)
     target = (finals * final_scale[:, None] * gain_cols).astype(jnp.bfloat16)
     slab_rows = unembed_full
-    logits = jnp.dot(
-        lax.all_gather(normed, "vocab", axis=1, tiled=True),
-        slab_rows,
-        preferred_element_type=jnp.float32,
-    )
+    logits = jnp.dot(modes_switch(normed), slab_rows, preferred_element_type=jnp.float32)
     target_logits = jnp.dot(
         lax.all_gather(target, "vocab", axis=1, tiled=True),
         slab_rows,

time: 1220 us -> 1080 us (0.89)
  waiting for transfers between devices: 482 us -> 340 us
    all_gather x1, waiting for transfers between devices: 91.2 us -> 0.01 us  [per_device(): unembed_full = lax.all_gather(unembed, 'section', axis=0, tiled=True)]
    all_gather x1 -> x0, waiting for transfers between devices: 90.7 us -> none  [per_device(): lax.all_gather(normed, 'vocab', axis=1, tiled=True)]
    all_to_all x0 -> x1, waiting for transfers between devices: none -> 36.8 us  [modes_switch(): lax.all_to_all(jnp.stack(lax.axis_size('vocab') * [body], 0), 'vocab', 0, 0)]
  transfers between devices with their start and end apart: 5 -> 5, of which waited for: 4 -> 3; matrix products, arithmetic and copies ran while one was open for 1% -> 1% of each run, Pallas kernels for 0% -> 0%
where the time goes in v1:
time: 1080 us
  blocking collectives  685 us (63%)
  waiting for transfers between devices  340 us (31%)
  matrix products  25.5 us (2%)
  between operations  15.6 us (1%)
    all_gather x4, blocking collectives, combined_all(): pieces = jax.tree.map(lambda part: lax.all_gather(part, axis), value)  438 us
    reduce_scatter x1, waiting for transfers between devices, per_device(): lax.psum_scatter(lax.dot_general(slab_rows, dlogits, (((1,), (1,)), ((),...  218 us
    psum x1, blocking collectives, per_device(): lax.psum(jnp.sum(scaled_cols * trans_cols, axis=0), 'vocab') / width  118 us
    psum x1, blocking collectives, per_device(): lax.psum((jnp.sum(trans * trans, axis=-1), jnp.sum(finals * finals, axis=...  112 us
    all_gather x1, waiting for transfers between devices, per_device(): inputs = lax.all_gather(input_cols, 'vocab', axis=1, tiled=True)  83.7 us
    all_to_all x1, waiting for transfers between devices, modes_switch(): lax.all_to_all(jnp.stack(lax.axis_size('vocab') * [body], 0), 'vocab', 0, 0)  36.8 us
  transfers between devices with their start and end apart: 5, of which 3 were waited for; matrix products, arithmetic and copies ran while one was open for 1% of the time, Pallas kernels for 0%

profile of v1, /device:TPU:2, one launch (start us, length us, event | category | flops | bytes accessed | tf_op | source)
XLA Modules:
  0.0 1081.8 jit_solution(18250232074506729812)
XLA Ops:
  7.2 0.0 copy-start
  7.2 0.0 all-gather.17.cloned.1.call-start
  7.2 0.7 fusion.34
  7.9 0.2 copy-done
  8.1 1.5 gather_fusion
  9.6 0.0 all-gather.17.cloned.1.call-update
  9.6 0.0 all-gather.13.cloned.1.call-start
  9.7 0.7 all-gather.13.cloned.1.call-update
  10.4 0.7 add.75
  11.1 15.4 %all_gather.42 = bf16[512,256]{1,0:T(8,128)(2,1)S(1)} all-gather(bf16[64,256]{1,0:T(8,128)(2,1)} %param.10), channel_id=1, replica_groups=mesh['section'=8,'vocab'=32] {'section'}, dimensions={0}, use_global_device_ids=true | all-gather | bytes 294912 | tf_op jit(solution)/shard_map/all_gather | solution.py:45
  26.4 0.8 gather_fusion.1
  27.3 0.7 convert_element_type.38
  27.9 0.1 fusion.20
  28.0 83.7 %all-gather.17.cloned.1.call-done = bf16[128,8192]{1,0:T(8,128)(2,1)} async-done(((bf16[128,256]{1,0:T(8,128)(2,1)}), bf16[128,8192]{1,0:T(8,128)(2,1)}) %all-gather.17.cloned.1.call-update) | async-done | bytes 2097168 | tf_op jit(solution)/shard_map/all_gather | solution.py:48
  111.8 3.7 multiply_reduce_fusion.1
  115.4 112.4 %all-reduce.1 = (f32[128]{0:T(128)S(1)}, f32[128]{0:T(128)S(1)}) all-reduce(f32[128]{0:T(128)S(1)} %fusion.20, f32[128]{0:T(128)S(1)} %get-tuple-element.87), channel_id=1, replica_groups=mesh['section'=8,'vocab'=32] {'vocab'}, use_global_device_ids=true, to_apply=%region_5.0 | all-reduce | flops 256 | bytes 2048 | tf_op jit(solution)/shard_map/psum | solution.py:55
  227.9 0.7 multiply_convert_fusion
  228.6 0.1 copy.11
  228.7 1.8 stack.8
  230.5 3.8 all-to-all-start
  234.3 0.0 all-gather.15.cloned.1.call-start
  234.4 0.7 all-gather.15.cloned.1.call-update
  235.1 0.0 reduce-scatter.2.cloned.1.call-start
  235.1 36.8 %all-to-all-done = bf16[32,128,256]{1,2,0:T(8,128)(2,1)S(1)} async-done(((bf16[32,128,256]{1,2,0:T(8,128)(2,1)}), bf16[32,128,256]{1,2,0:T(8,128)(2,1)S(1)}, u32[]{:S(2)}, u32[]{:S(2)}) %all-to-all-start) | async-done | bytes 2097184 | tf_op jit(solution)/shard_map/all_to_all | solution.py:38
  272.0 0.0 all-gather.13.cloned.1.call-done
  272.0 4.8 fusion.37
  276.7 0.2 exponential_reduce_fusion.1
  276.9 108.7 %all-gather.6 = f32[32,1,128]{2,1,0:T(1,128)S(1)} all-gather(f32[1,1,128]{2,1,0:T(1,128)S(1)} %bitcast.106), channel_id=4, replica_groups=mesh['section'=8,'vocab'=32] {'vocab'}, dimensions={0}, use_global_device_ids=true | all-gather | bytes 16896 | tf_op jit(solution)/shard_map/all_gather | solution.py:10
  385.6 0.0 all-gather.15.cloned.1.call-done
  385.6 5.4 fusion.38
  391.0 0.2 exponential_reduce_fusion
  391.2 114.5 %all-gather.8 = f32[32,1,128]{2,1,0:T(1,128)S(1)} all-gather(f32[1,1,128]{2,1,0:T(1,128)S(1)} %bitcast.107), channel_id=6, replica_groups=mesh['section'=8,'vocab'=32] {'vocab'}, dimensions={0}, use_global_device_ids=true | all-gather | bytes 16896 | tf_op jit(solution)/shard_map/all_gather | solution.py:10
  505.7 106.6 %all-gather.5 = f32[32,1,128]{2,1,0:T(1,128)S(1)} all-gather(f32[1,1,128]{2,1,0:T(1,128)S(1)} %bitcast.103), channel_id=3, replica_groups=mesh['section'=8,'vocab'=32] {'vocab'}, dimensions={0}, use_global_device_ids=true | all-gather | bytes 16896 | tf_op jit(solution)/shard_map/all_gather | solution.py:10
  612.3 108.6 %all-gather.7 = f32[32,1,128]{2,1,0:T(1,128)S(1)} all-gather(f32[1,1,128]{2,1,0:T(1,128)S(1)} %bitcast.104), channel_id=5, replica_groups=mesh['section'=8,'vocab'=32] {'vocab'}, dimensions={0}, use_global_device_ids=true | all-gather | bytes 16896 | tf_op jit(solution)/shard_map/all_gather | solution.py:10
  720.9 1.5 while.16
  722.4 7.5 fusion.11
  730.0 0.0 copy-start.1
  730.0 0.0 reduce-scatter.2.cloned.1.call-update
  730.0 0.2 multiply_reduce_fusion
  730.2 217.6 %reduce-scatter.2.cloned.1.call-done = bf16[256,128]{0,1:T(8,128)(2,1)} async-done(((bf16[8192,128]{0,1:T(8,128)(2,1)}), bf16[256,128]{0,1:T(8,128)(2,1)}) %reduce-scatter.2.cloned.1.call-update) | async-done | bytes 65552 | tf_op jit(solution)/shard_map/reduce_scatter | solution.py:79
  947.8 0.9 fusion.23
  948.8 118.4 %all-reduce = (f32[128]{0:T(128)S(1)}, f32[128]{0:T(128)S(1)}) all-reduce(f32[128]{0:T(128)S(1)} %fusion.23, f32[128]{0:T(128)S(1)} %multiply_reduce_fusion), channel_id=1, replica_groups=mesh['section'=8,'vocab'=32] {'vocab'}, use_global_device_ids=true, to_apply=%region_12.13 | all-reduce | flops 256 | bytes 2048 | tf_op jit(solution)/shard_map/psum | solution.py:89
  1067.2 0.6 reduce_sum.79
  1068.4 1.5 fusion.28
  1069.9 0.0 copy-done.1
  1069.9 4.2 fusion.10
  (48 shorter events, 1.1 us)
Async XLA Ops:
  7.2 1.0 copy-start
  7.2 104.6 %all-gather.17.cloned.1.call-start = ((), (), s32[]{:S(2)}) async-start(), calls=%async_computation.5 | async-start | bytes 2162688 | tf_op jit(solution)/shard_map/all_gather | solution.py:48
  9.6 262.3 %all-gather.13.cloned.1.call-start = ((), (), s32[]{:S(2)}) async-start(), calls=%async_computation.2 | async-start | bytes 9437184 | tf_op jit(solution)/shard_map/all_gather | solution.py:44
  230.5 41.4 %all-to-all-start = ((bf16[32,128,256]{1,2,0:T(8,128)(2,1)}), bf16[32,128,256]{1,2,0:T(8,128)(2,1)S(1)}, u32[]{:S(2)}, u32[]{:S(2)}) async-start(bf16[32,128,256]{1,2,0:T(8,128)(2,1)} %stack.8), calls=%async_computation | async-start | bytes 4194304 | tf_op jit(solution)/shard_map/all_to_all | solution.py:38
  234.3 151.3 %all-gather.15.cloned.1.call-start = ((), (), s32[]{:S(2)}) async-start(), calls=%async_computation.3 | async-start | bytes 2162688 | tf_op jit(solution)/shard_map/all_gather | solution.py:65
  235.1 712.7 %reduce-scatter.2.cloned.1.call-start = ((), (), s32[]{:S(2)}) async-start(), calls=%async_computation.4 | async-start | bytes 2162688 | tf_op jit(solution)/shard_map/reduce_scatter | solution.py:79
  730.0 340.0 %copy-start.1 = (bf16[128,8192]{1,0:T(8,128)(2,1)S(1)}, bf16[128,8192]{1,0:T(8,128)(2,1)}, u32[]{:S(2)}) copy-start(bf16[128,8192]{1,0:T(8,128)(2,1)} %all-gather.17.cloned.1.call-done) | copy-start | bytes 6291460
Sparse Core Ops, SparseCore 0:
  11.8 99.9 all-gather.16
  113.6 89.4 all-gather.12
  238.4 107.1 all-gather.14
  730.1 217.6 reduce-scatter.1
